TPU v7x, 128 devices: a whole 4x4x4 slice. The times are simulated.
128 devices in a mesh: section: 8 (over x_lo, z), tp: 16 (over y, x_hi, core).
Axes of the slice: x: 4 (x_hi: 2, x_lo: 2; x = x_hi * 2 + x_lo), y: 4, z: 4, core: 2. Of those that a mesh axis runs over, the one named last changes fastest.
Arguments:
- stash: bfloat16 [8, 4, 192, 1024], P('section', None, 'tp'), may hold values from -6 to 6
- w_in: bfloat16 [8, 1024, 65536], P('section', None, 'tp'), may hold values from -0.1875 to 0.1875
- w_out: bfloat16 [8, 65536, 1024], P('section', 'tp'), may hold values from -0.0234375 to 0.0234375
- gain: float32 [8, 1024], P('section'), may hold values from 0.1 to 1.9
- plan: int32 [3, 8], replicated, may hold values from 0 to 3
- arriving: bfloat16 [8, 192, 1024], P('section', 'tp'), may hold values from -6 to 6
- fresh: bfloat16 [2, 192, 1024], P(None, 'tp'), may hold values from -6 to 6
Outputs:
- input_grads: bfloat16 [3, 8, 192, 1024], P(None, 'section', 'tp')
All inputs are finite; a program needn't handle non-finite values.
Results may differ from a plain program's by a relative error of at most 0.0085.
Values may be sent and summed in bfloat16 or wider, within the bound.
A program may use at most 64 MiB of HBM per device.

v0:
```python
import jax
import jax.numpy as jnp
from jax import lax
from jax.sharding import PartitionSpec as P

epsilon = 1e-06
contract_last = (((1,), (1,)), ((), ()))


def from_partner(value, axis, apart):
    return lax.ppermute(value, axis, [(i, i ^ 1 << apart) for i in range(lax.axis_size(axis))])


def sent_to_all(value, axis):
    copies = jnp.broadcast_to(value, (lax.axis_size(axis), *value.shape))
    return lax.all_to_all(copies, axis, split_axis=0, concat_axis=0, tiled=True)


def joined_along(blocks, dim):
    shape = list(blocks.shape[1:])
    shape[dim] *= blocks.shape[0]
    return jnp.moveaxis(blocks, 0, dim).reshape(shape)


def gathered_copies(value, axis, dim):
    blocks = sent_to_all(value, axis)
    return joined_along(blocks, dim)


def in_blocks(value, dim, devices):
    shape = value.shape
    blocks = value.reshape(*shape[:dim], devices, shape[dim] // devices, *shape[dim + 1 :])
    return jnp.moveaxis(blocks, dim, 0)


def sum_at_owner(value, axis, dim):
    devices = lax.axis_size(axis)
    blocks = lax.all_to_all(in_blocks(value, dim, devices), axis, 0, 0, tiled=True)
    return jnp.sum(blocks, axis=0)


def shifted(value, axis, steps):
    count = lax.axis_size(axis)
    first, last = (max(0, -steps), min(count, count - steps))
    return lax.ppermute(value, axis, [(source, source + steps) for source in range(first, last)])


def norm_parts(x_rows):
    values = x_rows.astype(jnp.float32)
    inverse_rms = lax.rsqrt(jnp.mean(values * values, axis=-1, keepdims=True) + epsilon)
    return (inverse_rms, values * inverse_rms)


def norm_back(normed_grad, incoming, inverse_rms, normed, gain_row):
    scaled = normed_grad * gain_row
    inner = jnp.mean(scaled * normed, axis=-1, keepdims=True)
    return (incoming.astype(jnp.float32) + inverse_rms * (scaled - normed * inner)).astype(
        jnp.bfloat16
    )


def body(stash, w_in, w_out, gain, plan, arriving, fresh):
    section_index = lax.axis_index("section")
    section_total = lax.axis_size("section")
    half_bit = section_total.bit_length() - 2
    tp_index = lax.axis_index("tp")
    stored = stash[0]
    weight_in = w_in[0]
    weight_out = w_out[0]
    gain_row = gain[0]
    row_count = stored.shape[1]
    ticks = plan.shape[0]
    partner = (section_index + section_total // 2) % section_total
    is_last = section_index == section_total - 1
    offset = tp_index * row_count
    slot_list = lax.dynamic_index_in_dim(plan, partner, 1, keepdims=False)
    picks_all = stored[slot_list]
    received_all = from_partner(picks_all, "section", half_bit)
    full_all = gathered_copies(received_all, "tp", 1)
    incoming_shard = arriving[0]
    results = []
    for tick in range(ticks):
        full_rows = full_all[tick]
        inverse_rms, normed = norm_parts(full_rows)
        inputs = (normed * gain_row).astype(jnp.bfloat16)
        preact = jnp.dot(inputs, weight_in, preferred_element_type=jnp.float32)
        incoming = gathered_copies(incoming_shard, "tp", 0)
        hidden_back = lax.dot_general(
            incoming, weight_out, contract_last, preferred_element_type=jnp.float32
        )
        hidden_grad = (hidden_back * (2.0 * jnp.maximum(preact, 0.0))).astype(jnp.bfloat16)
        normed_grad = sum_at_owner(
            lax.dot_general(
                hidden_grad, weight_in, contract_last, preferred_element_type=jnp.float32
            ),
            "tp",
            0,
        )
        own_rms = lax.dynamic_slice_in_dim(inverse_rms, offset, row_count, 0)
        own_normed = lax.dynamic_slice_in_dim(normed, offset, row_count, 0)
        outgoing = norm_back(normed_grad, incoming_shard, own_rms, own_normed, gain_row)
        results.append(outgoing)
        if tick + 1 < ticks:
            below = shifted(outgoing, "section", -1)
            incoming_shard = jnp.where(is_last, fresh[tick], below)
    return jnp.stack(results)[:, None]


def solution(mesh):
    placed = (
        P("section", None, "tp", None),
        P("section", None, "tp"),
        P("section", "tp", None),
        P("section", None),
        P(),
        P("section", "tp", None),
        P(None, "tp", None),
    )
    return jax.shard_map(
        body, mesh=mesh, in_specs=placed, out_specs=P(None, "section", "tp", None), check_vma=False
    )
```

profile of v0, /device:TPU:96, one launch (start us, length us, event | category | flops | bytes accessed | tf_op | source)
XLA Modules:
  0.0 222.4 jit_solution(15740418765718681253)
XLA Ops:
  0.0 1.6 broadcast_in_dim.11
  1.6 7.0 %all-to-all-start.1 = ((bf16[16,12,1024]{2,1,0:T(8,128)(2,1)}), bf16[16,12,1024]{2,1,0:T(8,128)(2,1)S(1)}, u32[]{:S(2)}, u32[]{:S(2)}) async-start(bf16[16,12,1024]{2,1,0:T(8,128)(2,1)} %broadcast_in_dim.11), calls=%async_computation.1 | async-start | bytes 1048576 | tf_op jit(solution)/shard_map/all_to_all | solution.py:16
  11.7 6.7 %collective-permute-done = bf16[3,12,1024]{2,1,0:T(8,128)(2,1)S(1)} collective-permute-done((bf16[3,12,1024]{2,1,0:T(8,128)(2,1)S(1)}, bf16[3,12,1024]{2,1,0:T(8,128)(2,1)S(1)}, u32[]{:S(2)}, u32[]{:S(2)}) %collective-permute-start) | collective-permute-done | bytes 73760 | tf_op jit(solution)/shard_map/ppermute | solution.py:11
  18.4 3.1 %all-to-all-done.1 = bf16[16,12,1024]{2,1,0:T(8,128)(2,1)S(1)} async-done(((bf16[16,12,1024]{2,1,0:T(8,128)(2,1)}), bf16[16,12,1024]{2,1,0:T(8,128)(2,1)S(1)}, u32[]{:S(2)}, u32[]{:S(2)}) %all-to-all-start.1) | async-done | bytes 393248 | tf_op jit(solution)/shard_map/all_to_all | solution.py:16
  22.9 4.5 %all-to-all-start = ((bf16[16,3,12,1024]{3,2,1,0:T(8,128)(2,1)}), bf16[16,3,12,1024]{3,2,1,0:T(8,128)(2,1)S(1)}, u32[]{:S(2)}, u32[]{:S(2)}) async-start(bf16[16,3,12,1024]{3,2,1,0:T(8,128)(2,1)} %broadcast_in_dim.10), calls=%async_computation | async-start | bytes 3145728 | tf_op jit(solution)/shard_map/all_to_all | solution.py:16
  27.5 23.6 %all-to-all-done = bf16[16,3,12,1024]{3,2,1,0:T(8,128)(2,1)S(1)} async-done(((bf16[16,3,12,1024]{3,2,1,0:T(8,128)(2,1)}), bf16[16,3,12,1024]{3,2,1,0:T(8,128)(2,1)S(1)}, u32[]{:S(2)}, u32[]{:S(2)}) %all-to-all-start) | async-done | bytes 1179680 | tf_op jit(solution)/shard_map/all_to_all | solution.py:16
  53.1 5.2 %fusion.42 = f32[192,4096]{1,0:T(8,128)S(1)} fusion(bf16[192,1024]{1,0:T(8,128)(2,1)S(1)} %convert_element_type.78, bf16[1,1024,4096]{2,1,0:T(8,128)(2,1)} %param.8), kind=kOutput, calls=%fused_computation.27 | convolution fusion | flops 1612185600 | bytes 11927552 | tf_op jit(solution)/shard_map/dot_general | solution.py:86
  58.3 6.3 %fusion.51 = bf16[192,4096]{1,0:T(8,128)(2,1)S(1)} fusion(f32[192,4096]{1,0:T(8,128)S(1)} %fusion.42, bf16[192,1024]{1,0:T(8,128)(2,1)S(1)} %reshape.175, bf16[1,4096,1024]{2,1,0:T(8,128)(2,1)} %param.9), kind=kOutput, calls=%fused_computation.30 | convolution fusion | flops 1612185600 | bytes 13500416 | tf_op jit(solution)/shard_map/dot_general | solution.py:88
  64.6 1.5 dot_general.35
  66.2 7.4 %fusion.4 = f32[16,12,1024]{2,1,0:T(8,128)} fusion(bf16[16,12,4096]{2,1,0:T(8,128)(2,1)} %dot_general.35, bf16[1,1024,4096]{2,1,0:T(8,128)(2,1)} %param.8), kind=kOutput, calls=%fused_computation.5 | convolution fusion | flops 1610612736 | bytes 10747904 | tf_op jit(solution)/shard_map/dot_general | solution.py:93
  73.6 3.7 %all-to-all-start.2 = ((f32[16,12,1024]{2,1,0:T(8,128)}), f32[16,12,1024]{2,1,0:T(8,128)S(1)}, u32[]{:S(2)}, u32[]{:S(2)}) async-start(f32[16,12,1024]{2,1,0:T(8,128)} %fusion.4), calls=%async_computation.2 | async-start | bytes 2097152 | tf_op jit(solution)/shard_map/all_to_all | solution.py:38
  77.5 1.7 slice_convert_fusion.1
  80.7 14.5 %all-to-all-done.2 = f32[16,12,1024]{2,1,0:T(8,128)S(1)} async-done(((f32[16,12,1024]{2,1,0:T(8,128)}), f32[16,12,1024]{2,1,0:T(8,128)S(1)}, u32[]{:S(2)}, u32[]{:S(2)}) %all-to-all-start.2) | async-done | bytes 786464 | tf_op jit(solution)/shard_map/all_to_all | solution.py:38
  95.6 2.3 %collective-permute-start.1 = (bf16[12,1024]{1,0:T(8,128)(2,1)S(1)}, bf16[12,1024]{1,0:T(8,128)(2,1)S(1)}, u32[]{:S(2)}, u32[]{:S(2)}) collective-permute-start(bf16[12,1024]{1,0:T(8,128)(2,1)S(1)} %add_convert_fusion.2), channel_id=1, source_target_pairs={{16,0},{32,16},{48,32},{64,48},{80,64},{96,80},{112,96},{17,1},{33... | collective-permute-start | bytes 73736 | tf_op jit(solution)/shard_map/ppermute | solution.py:45
  98.1 5.4 %collective-permute-done.1 = bf16[12,1024]{1,0:T(8,128)(2,1)S(1)} collective-permute-done((bf16[12,1024]{1,0:T(8,128)(2,1)S(1)}, bf16[12,1024]{1,0:T(8,128)(2,1)S(1)}, u32[]{:S(2)}, u32[]{:S(2)}) %collective-permute-start.1) | collective-permute-done | bytes 24608 | tf_op jit(solution)/shard_map/ppermute | solution.py:45
  104.3 3.8 %all-to-all-start.3 = ((bf16[16,12,1024]{2,1,0:T(8,128)(2,1)}), bf16[16,12,1024]{2,1,0:T(8,128)(2,1)S(1)}, u32[]{:S(2)}, u32[]{:S(2)}) async-start(bf16[16,12,1024]{2,1,0:T(8,128)(2,1)} %broadcast_in_dim.24), calls=%async_computation.3 | async-start | bytes 1048576 | tf_op jit(solution)/shard_map/all_to_all | solution.py:16
  108.1 6.9 %fusion.36 = f32[192,4096]{1,0:T(8,128)} fusion(bf16[192,1024]{1,0:T(8,128)(2,1)S(1)} %convert_element_type.86, bf16[1,1024,4096]{2,1,0:T(8,128)(2,1)} %param.8), kind=kOutput, calls=%fused_computation.25 | convolution fusion | flops 1612185600 | bytes 11927552 | tf_op jit(solution)/shard_map/dot_general | solution.py:86
  115.0 5.2 %all-to-all-done.3 = bf16[16,12,1024]{2,1,0:T(8,128)(2,1)S(1)} async-done(((bf16[16,12,1024]{2,1,0:T(8,128)(2,1)}), bf16[16,12,1024]{2,1,0:T(8,128)(2,1)S(1)}, u32[]{:S(2)}, u32[]{:S(2)}) %all-to-all-start.3) | async-done | bytes 393248 | tf_op jit(solution)/shard_map/all_to_all | solution.py:16
  120.3 7.2 %fusion.48 = bf16[192,4096]{1,0:T(8,128)(2,1)S(1)} fusion(f32[192,4096]{1,0:T(8,128)} %fusion.36, bf16[192,1024]{1,0:T(8,128)(2,1)S(1)} %reshape.176, bf16[1,4096,1024]{2,1,0:T(8,128)(2,1)} %param.9), kind=kOutput, calls=%fused_computation.29 | convolution fusion | flops 1612185600 | bytes 13500416 | tf_op jit(solution)/shard_map/dot_general | solution.py:88
  127.5 1.5 dot_general.39
  129.1 7.4 %fusion.2 = f32[16,12,1024]{2,1,0:T(8,128)} fusion(bf16[16,12,4096]{2,1,0:T(8,128)(2,1)} %dot_general.39, bf16[1,1024,4096]{2,1,0:T(8,128)(2,1)} %param.8), kind=kOutput, calls=%fused_computation.3 | convolution fusion | flops 1610612736 | bytes 10747904 | tf_op jit(solution)/shard_map/dot_general | solution.py:93
  136.5 3.8 %all-to-all-start.4 = ((f32[16,12,1024]{2,1,0:T(8,128)}), f32[16,12,1024]{2,1,0:T(8,128)S(1)}, u32[]{:S(2)}, u32[]{:S(2)}) async-start(f32[16,12,1024]{2,1,0:T(8,128)} %fusion.2), calls=%async_computation.4 | async-start | bytes 2097152 | tf_op jit(solution)/shard_map/all_to_all | solution.py:38
  140.7 17.5 %all-to-all-done.4 = f32[16,12,1024]{2,1,0:T(8,128)S(1)} async-done(((f32[16,12,1024]{2,1,0:T(8,128)}), f32[16,12,1024]{2,1,0:T(8,128)S(1)}, u32[]{:S(2)}, u32[]{:S(2)}) %all-to-all-start.4) | async-done | bytes 786464 | tf_op jit(solution)/shard_map/all_to_all | solution.py:38
  158.6 1.9 collective-permute-start.2
  160.7 5.9 %collective-permute-done.2 = bf16[12,1024]{1,0:T(8,128)(2,1)S(1)} collective-permute-done((bf16[12,1024]{1,0:T(8,128)(2,1)S(1)}, bf16[12,1024]{1,0:T(8,128)(2,1)S(1)}, u32[]{:S(2)}, u32[]{:S(2)}) %collective-permute-start.2) | collective-permute-done | bytes 24608 | tf_op jit(solution)/shard_map/ppermute | solution.py:45
  167.4 3.8 %all-to-all-start.5 = ((bf16[16,12,1024]{2,1,0:T(8,128)(2,1)}), bf16[16,12,1024]{2,1,0:T(8,128)(2,1)S(1)}, u32[]{:S(2)}, u32[]{:S(2)}) async-start(bf16[16,12,1024]{2,1,0:T(8,128)(2,1)} %broadcast_in_dim.25), calls=%async_computation.5 | async-start | bytes 1048576 | tf_op jit(solution)/shard_map/all_to_all | solution.py:16
  171.2 6.9 %fusion.39 = f32[192,4096]{1,0:T(8,128)} fusion(bf16[192,1024]{1,0:T(8,128)(2,1)S(1)} %convert_element_type.94, bf16[1,1024,4096]{2,1,0:T(8,128)(2,1)} %param.8), kind=kOutput, calls=%fused_computation.26 | convolution fusion | flops 1612185600 | bytes 11927552 | tf_op jit(solution)/shard_map/dot_general | solution.py:86
  178.1 5.2 %all-to-all-done.5 = bf16[16,12,1024]{2,1,0:T(8,128)(2,1)S(1)} async-done(((bf16[16,12,1024]{2,1,0:T(8,128)(2,1)}), bf16[16,12,1024]{2,1,0:T(8,128)(2,1)S(1)}, u32[]{:S(2)}, u32[]{:S(2)}) %all-to-all-start.5) | async-done | bytes 393248 | tf_op jit(solution)/shard_map/all_to_all | solution.py:16
  183.4 7.2 %fusion.45 = bf16[192,4096]{1,0:T(8,128)(2,1)S(1)} fusion(f32[192,4096]{1,0:T(8,128)} %fusion.39, bf16[192,1024]{1,0:T(8,128)(2,1)S(1)} %reshape.177, bf16[1,4096,1024]{2,1,0:T(8,128)(2,1)} %param.9), kind=kOutput, calls=%fused_computation.28 | convolution fusion | flops 1612185600 | bytes 13500416 | tf_op jit(solution)/shard_map/dot_general | solution.py:88
  192.1 7.5 %fusion = f32[16,12,1024]{2,1,0:T(8,128)} fusion(bf16[16,12,4096]{2,1,0:T(8,128)(2,1)} %dot_general.43, bf16[1,1024,4096]{2,1,0:T(8,128)(2,1)} %param.8), kind=kOutput, calls=%fused_computation.1 | convolution fusion | flops 1610612736 | bytes 10747904 | tf_op jit(solution)/shard_map/dot_general | solution.py:93
  199.6 3.8 %all-to-all-start.6 = ((f32[16,12,1024]{2,1,0:T(8,128)}), f32[16,12,1024]{2,1,0:T(8,128)S(1)}, u32[]{:S(2)}, u32[]{:S(2)}) async-start(f32[16,12,1024]{2,1,0:T(8,128)} %fusion), calls=%async_computation.6 | async-start | bytes 2097152 | tf_op jit(solution)/shard_map/all_to_all | solution.py:38
  203.8 17.5 %all-to-all-done.6 = f32[16,12,1024]{2,1,0:T(8,128)S(1)} async-done(((f32[16,12,1024]{2,1,0:T(8,128)}), f32[16,12,1024]{2,1,0:T(8,128)S(1)}, u32[]{:S(2)}, u32[]{:S(2)}) %all-to-all-start.6) | async-done | bytes 786464 | tf_op jit(solution)/shard_map/all_to_all | solution.py:38
  (76 shorter events, 14.3 us)
Async XLA Ops:
  1.6 19.9 %all-to-all-start.1 = ((bf16[16,12,1024]{2,1,0:T(8,128)(2,1)}), bf16[16,12,1024]{2,1,0:T(8,128)(2,1)S(1)}, u32[]{:S(2)}, u32[]{:S(2)}) async-start(bf16[16,12,1024]{2,1,0:T(8,128)(2,1)} %broadcast_in_dim.11), calls=%async_computation.1 | async-start | bytes 1048576 | tf_op jit(solution)/shard_map/all_to_all | solution.py:16
  11.0 7.4 %collective-permute-start = (bf16[3,12,1024]{2,1,0:T(8,128)(2,1)S(1)}, bf16[3,12,1024]{2,1,0:T(8,128)(2,1)S(1)}, u32[]{:S(2)}, u32[]{:S(2)}) collective-permute-start(bf16[3,12,1024]{2,1,0:T(8,128)(2,1)S(1)} %gather_fusion), channel_id=1, source_target_pairs={{0,64},{16,80},{32,96},{48,112},{64,0},{80,16},{96,32},{112,48},{1... | collective-permute-start | bytes 221192 | tf_op jit(solution)/shard_map/ppermute | solution.py:11
  22.9 28.7 %copy-start.4 = (f32[1,1024]{1,0:T(1,128)S(1)}, f32[1,1024]{1,0:T(1,128)}, u32[]{:S(2)}) copy-start(f32[1,1024]{1,0:T(1,128)} %param.10) | copy-start | bytes 12292
  22.9 28.2 %all-to-all-start = ((bf16[16,3,12,1024]{3,2,1,0:T(8,128)(2,1)}), bf16[16,3,12,1024]{3,2,1,0:T(8,128)(2,1)S(1)}, u32[]{:S(2)}, u32[]{:S(2)}) async-start(bf16[16,3,12,1024]{3,2,1,0:T(8,128)(2,1)} %broadcast_in_dim.10), calls=%async_computation | async-start | bytes 3145728 | tf_op jit(solution)/shard_map/all_to_all | solution.py:16
  51.5 1.4 copy-start.8
  51.6 1.4 copy-start.6
  66.2 11.1 %copy-start.9 = (f32[16,12]{1,0:T(8,128)S(1)}, f32[16,12]{1,0:T(8,128)}, u32[]{:S(2)}) copy-start(f32[16,12]{1,0:T(8,128)} %copy-done.8) | copy-start | bytes 2308
  73.6 21.6 %all-to-all-start.2 = ((f32[16,12,1024]{2,1,0:T(8,128)}), f32[16,12,1024]{2,1,0:T(8,128)S(1)}, u32[]{:S(2)}, u32[]{:S(2)}) async-start(f32[16,12,1024]{2,1,0:T(8,128)} %fusion.4), calls=%async_computation.2 | async-start | bytes 2097152 | tf_op jit(solution)/shard_map/all_to_all | solution.py:38
  77.4 18.0 %copy-start.10 = (bf16[1,12,1024]{2,1,0:T(8,128)(2,1)S(1)}, bf16[1,12,1024]{2,1,0:T(8,128)(2,1)}, u32[]{:S(2)}) copy-start(bf16[1,12,1024]{2,1,0:T(8,128)(2,1)} %param.12) | copy-start | bytes 73732
  77.4 20.4 %copy-start.5 = (bf16[2,12,1024]{2,0,1:T(2,128)(2,1)S(1)}, bf16[2,12,1024]{2,0,1:T(2,128)(2,1)}, u32[]{:S(2)}) copy-start(bf16[2,12,1024]{2,0,1:T(2,128)(2,1)} %param.13) | copy-start | bytes 147460
  77.5 20.5 %copy-start.3 = (bf16[1,16,12,1024]{3,2,0,1:T(8,128)(2,1)S(1)}, bf16[1,16,12,1024]{3,2,0,1:T(8,128)(2,1)}, u32[]{:S(2)}) copy-start(bf16[1,16,12,1024]{3,2,0,1:T(8,128)(2,1)} %get-tuple-element.8) | copy-start | bytes 1179652
  95.6 19.4 %copy-start.11 = (bf16[12,1024]{1,0:T(8,128)(2,1)}, bf16[12,1024]{1,0:T(8,128)(2,1)S(1)}, u32[]{:S(2)}) copy-start(bf16[12,1024]{1,0:T(8,128)(2,1)S(1)} %add_convert_fusion.2) | copy-start | bytes 73732
  95.6 7.9 %collective-permute-start.1 = (bf16[12,1024]{1,0:T(8,128)(2,1)S(1)}, bf16[12,1024]{1,0:T(8,128)(2,1)S(1)}, u32[]{:S(2)}, u32[]{:S(2)}) collective-permute-start(bf16[12,1024]{1,0:T(8,128)(2,1)S(1)} %add_convert_fusion.2), channel_id=1, source_target_pairs={{16,0},{32,16},{48,32},{64,48},{80,64},{96,80},{112,96},{17,1},{33... | collective-permute-start | bytes 73736 | tf_op jit(solution)/shard_map/ppermute | solution.py:45
  104.3 15.9 %all-to-all-start.3 = ((bf16[16,12,1024]{2,1,0:T(8,128)(2,1)}), bf16[16,12,1024]{2,1,0:T(8,128)(2,1)S(1)}, u32[]{:S(2)}, u32[]{:S(2)}) async-start(bf16[16,12,1024]{2,1,0:T(8,128)(2,1)} %broadcast_in_dim.24), calls=%async_computation.3 | async-start | bytes 1048576 | tf_op jit(solution)/shard_map/all_to_all | solution.py:16
  129.0 11.3 %copy-start.7 = (f32[16,12]{1,0:T(8,128)S(1)}, f32[16,12]{1,0:T(8,128)}, u32[]{:S(2)}) copy-start(f32[16,12]{1,0:T(8,128)} %copy-done.6) | copy-start | bytes 2308
  129.1 11.4 %copy-start.1 = (f32[1,16,12,1024]{3,2,0,1:T(8,128)S(1)}, f32[1,16,12,1024]{3,2,0,1:T(8,128)}, u32[]{:S(2)}) copy-start(f32[1,16,12,1024]{3,2,0,1:T(8,128)} %get-tuple-element.11) | copy-start | bytes 2359300
  136.5 24.0 %copy-start.2 = (bf16[1,16,12,1024]{3,2,0,1:T(8,128)(2,1)S(1)}, bf16[1,16,12,1024]{3,2,0,1:T(8,128)(2,1)}, u32[]{:S(2)}) copy-start(bf16[1,16,12,1024]{3,2,0,1:T(8,128)(2,1)} %get-tuple-element.9) | copy-start | bytes 1179652
  136.5 21.8 %all-to-all-start.4 = ((f32[16,12,1024]{2,1,0:T(8,128)}), f32[16,12,1024]{2,1,0:T(8,128)S(1)}, u32[]{:S(2)}, u32[]{:S(2)}) async-start(f32[16,12,1024]{2,1,0:T(8,128)} %fusion.2), calls=%async_computation.4 | async-start | bytes 2097152 | tf_op jit(solution)/shard_map/all_to_all | solution.py:38
  158.6 7.9 %collective-permute-start.2 = (bf16[12,1024]{1,0:T(8,128)(2,1)S(1)}, bf16[12,1024]{1,0:T(8,128)(2,1)S(1)}, u32[]{:S(2)}, u32[]{:S(2)}) collective-permute-start(bf16[12,1024]{1,0:T(8,128)(2,1)S(1)} %add_convert_fusion.1), channel_id=1, source_target_pairs={{16,0},{32,16},{48,32},{64,48},{80,64},{96,80},{112,96},{17,1},{33... | collective-permute-start | bytes 73736 | tf_op jit(solution)/shard_map/ppermute | solution.py:45
  167.4 15.9 %all-to-all-start.5 = ((bf16[16,12,1024]{2,1,0:T(8,128)(2,1)}), bf16[16,12,1024]{2,1,0:T(8,128)(2,1)S(1)}, u32[]{:S(2)}, u32[]{:S(2)}) async-start(bf16[16,12,1024]{2,1,0:T(8,128)(2,1)} %broadcast_in_dim.25), calls=%async_computation.5 | async-start | bytes 1048576 | tf_op jit(solution)/shard_map/all_to_all | solution.py:16
  192.1 11.4 %copy-start = (f32[1,16,12,1024]{3,2,0,1:T(8,128)S(1)}, f32[1,16,12,1024]{3,2,0,1:T(8,128)}, u32[]{:S(2)}) copy-start(f32[1,16,12,1024]{3,2,0,1:T(8,128)} %get-tuple-element.12) | copy-start | bytes 2359300
  199.6 22.1 %copy-start.12 = (bf16[12,1024]{1,0:T(8,128)(2,1)S(1)}, bf16[12,1024]{1,0:T(8,128)(2,1)}, u32[]{:S(2)}) copy-start(bf16[12,1024]{1,0:T(8,128)(2,1)} %copy-done.11) | copy-start | bytes 73732
  199.6 21.8 %all-to-all-start.6 = ((f32[16,12,1024]{2,1,0:T(8,128)}), f32[16,12,1024]{2,1,0:T(8,128)S(1)}, u32[]{:S(2)}, u32[]{:S(2)}) async-start(f32[16,12,1024]{2,1,0:T(8,128)} %fusion), calls=%async_computation.6 | async-start | bytes 2097152 | tf_op jit(solution)/shard_map/all_to_all | solution.py:38
where the time goes:
time: 224 us; the launch traced here: 222 us
  waiting for transfers between devices  105 us (47%)
  matrix products  62 us (28%)
  starting transfers between devices  35.2 us (16%)
  local copies, waits for them, and re-layouts  13.9 us (6%)
  other arithmetic  6.16 us (3%)
    all_to_all x3, waiting for transfers between devices, sum_at_owner(): lax.all_to_all(in_blocks(value, dim, devices), axis, 0, 0, tiled=True)  49.6 us
    all_to_all x4, waiting for transfers between devices, sent_to_all(): return lax.all_to_all(copies, axis, split_axis=0, concat_axis=0, tiled=True)  37.1 us
    dot_general x3, matrix products, body(): lax.dot_general(hidden_grad, weight_in, contract_last, preferred_element_...  22.3 us
    dot_general x3, matrix products, body(): lax.dot_general(incoming, weight_out, contract_last, preferred_element_ty...  20.7 us
    all_to_all x4, starting transfers between devices, sent_to_all(): return lax.all_to_all(copies, axis, split_axis=0, concat_axis=0, tiled=True)  19.1 us
    dot_general x3, matrix products, body(): preact = jnp.dot(inputs, weight_in, preferred_element_type=jnp.float32)  19 us
    ppermute x2, waiting for transfers between devices, shifted(): lax.ppermute(value, axis, [(source, source + steps) for source in range(f...  11.3 us
    all_to_all x3, starting transfers between devices, sum_at_owner(): lax.all_to_all(in_blocks(value, dim, devices), axis, 0, 0, tiled=True)  11.2 us
  transfers between devices with their start and end apart: 10, of which 10 were waited for; matrix products, arithmetic and copies ran while one was open for 9% of the time, Pallas kernels for 0%

commit v1 on v0

v1 whole, which is shorter than its diff:
```python
import functools

import jax
import jax.numpy as jnp
from jax import lax
from jax.experimental import pallas as pl
from jax.experimental.pallas import tpu as pltpu
from jax.sharding import PartitionSpec as P

epsilon = 1e-06
contract_last = (((1,), (1,)), ((), ()))
bf16, f32 = jnp.bfloat16, jnp.float32
PAD = 16
IN_TILE = 512
OUT_TILE = 256


def norm_parts(x_rows):
    values = x_rows.astype(f32)
    inverse_rms = lax.rsqrt(jnp.mean(values * values, axis=-1, keepdims=True) + epsilon)
    return inverse_rms, values * inverse_rms


def window_kernel(
    sections, tps, ticks,
    plan, stash, w_in, w_out, gain, arriving, fresh, out,
    wi, wo, stash_v, own, picks, x_all, inc_all, factor, hidden, acc, part, core_in, half, rs_in, out_v, up,
    load_sem, x_send, x_recv, xf_send, xf_recv, ag_send, ag_recv, agf_send, agf_recv,
    core_send, core_recv, rs_send, rs_recv, up_send, up_recv,
):
    section = lax.axis_index("section")
    me = lax.axis_index("tp")
    core = lax.rem(me, 2)
    place = me // 2
    places = tps // 2
    rows = stash.shape[1]
    width = stash.shape[2]
    units = wo.shape[0]
    mirror = lax.rem(section + sections // 2, sections)
    above = lax.rem(section + 1, sections)
    below = lax.rem(section + sections - 1, sections)
    mine = pl.multiple_of(core * places, places)
    theirs = pl.multiple_of((1 - core) * places, places)
    partner = me + 1 - 2 * core

    def remote(src, dst, send, recv, to_section, to_tp):
        return pltpu.make_async_remote_copy(
            src_ref=src, dst_ref=dst, send_sem=send, recv_sem=recv,
            device_id={"section": to_section, "tp": to_tp}, device_id_type=pl.DeviceIdType.MESH)

    def wait_for(ref, sem):
        pltpu.make_async_copy(ref, ref, sem).wait()

    def other_place(k):
        return lax.bitwise_xor(place, k)

    loads = [
        pltpu.make_async_copy(stash, stash_v, load_sem.at[0]),
        pltpu.make_async_copy(w_in, wi, load_sem.at[1]),
        pltpu.make_async_copy(w_out, wo, load_sem.at[2]),
    ]
    for load in loads:
        load.start()

    barrier = pltpu.get_barrier_semaphore()

    def greet(to_section, to_tp):
        pl.semaphore_signal(barrier, inc=1, device_id={"section": to_section, "tp": to_tp},
                            device_id_type=pl.DeviceIdType.MESH)

    greet(section, partner)
    for k in range(1, places):
        greet(section, other_place(k) * 2 + core)
    for k in range(places):
        greet(mirror, other_place(k) * 2 + core)
    greet(above, me)
    greet(below, me)

    own[...] = jnp.zeros_like(own)
    picks[...] = jnp.zeros_like(picks)
    own[0, 0:rows] = arriving[...]
    loads[0].wait()
    for t in range(ticks):
        picks[t, 0:rows] = stash_v[plan[t, mirror]]
    pl.semaphore_wait(barrier, 2 * places + 2)

    def send_x(t):
        for k in range(places):
            remote(picks.at[t], x_all.at[t, mine + place], x_send.at[t], x_recv.at[t],
                   mirror, other_place(k) * 2 + core).start()

    def send_incoming(t, src):
        pltpu.make_async_copy(src, inc_all.at[t, mine + place], ag_recv.at[t]).start()
        for k in (2, 6, 4, 1, 3, 7, 5):
            remote(src, inc_all.at[t, mine + place], ag_send.at[t], ag_recv.at[t],
                   section, other_place(k) * 2 + core).start()

    def forward(buf, t, recv, f_send, f_recv):
        block = buf.at[t, pl.ds(mine, places)]
        wait_for(block, recv.at[t])
        remote(block, block, f_send.at[t], f_recv.at[t], section, partner).start()

    def forwarded(buf, t, f_send, f_recv):
        wait_for(buf.at[t, pl.ds(mine, places)], f_send.at[t])
        wait_for(buf.at[t, pl.ds(theirs, places)], f_recv.at[t])

    gain_row = gain[...]

    def preact(t):
        forwarded(x_all, t, xf_send, xf_recv)
        _, normed = norm_parts(x_all[t].reshape(tps * PAD, width))
        inputs = (normed * gain_row).astype(bf16)

        def step(n, carry):
            cols = pl.ds(pl.multiple_of(n * IN_TILE, IN_TILE), IN_TILE)
            pre = jnp.dot(inputs, wi[:, cols], preferred_element_type=f32)
            factor[t, :, cols] = 2.0 * jnp.maximum(pre, 0.0)
            return carry

        lax.fori_loop(0, units // IN_TILE, step, 0)

    send_x(0)
    send_incoming(0, own.at[0])
    for t in range(1, ticks):
        send_x(t)
    for t in range(ticks - 1):
        own[t + 1, 0:rows] = fresh[t]
    loads[1].wait()
    loads[2].wait()
    forward(x_all, 0, x_recv, xf_send, xf_recv)
    forward(inc_all, 0, ag_recv, agf_send, agf_recv)
    preact(0)

    for t in range(ticks):
        forwarded(inc_all, t, agf_send, agf_recv)
        incoming = inc_all[t].reshape(tps * PAD, width)

        def up_step(n, carry):
            cols = pl.ds(pl.multiple_of(n * IN_TILE, IN_TILE), IN_TILE)
            back = lax.dot_general(incoming, wo[cols, :], contract_last, preferred_element_type=f32)
            hidden[:, cols] = (back * factor[t, :, cols]).astype(bf16)
            return carry

        lax.fori_loop(0, units // IN_TILE, up_step, 0)

        def down_step(n, carry):
            cols = pl.ds(pl.multiple_of(n * OUT_TILE, OUT_TILE), OUT_TILE)
            total = lax.dot_general(hidden[...], wi[cols, :], contract_last, preferred_element_type=f32)
            total = total.reshape(tps, PAD, OUT_TILE)
            acc[:, :, cols] = total
            part[t, :, :, cols] = total.astype(bf16)
            return carry

        lax.fori_loop(0, width // OUT_TILE, down_step, 0)
        remote(part.at[t, pl.ds(theirs, places)], core_in.at[t], core_send.at[t], core_recv.at[t],
               section, partner).start()
        wait_for(core_in.at[t], core_recv.at[t])
        half[t] = (acc[pl.ds(mine, places)] + core_in[t].astype(f32)).astype(bf16)
        for k in (6, 7, 4, 5, 2, 3, 1):
            remote(half.at[t, other_place(k)], rs_in.at[t, k - 1], rs_send.at[t], rs_recv.at[t],
                   section, other_place(k) * 2 + core).start()
        if t + 1 < ticks:
            forward(x_all, t + 1, x_recv, xf_send, xf_recv)
            preact(t + 1)
        inverse_rms, normed = norm_parts(x_all[t, mine + place])
        incoming_own = own[t].astype(f32)
        total = acc[mine + place] + core_in[t, place].astype(f32)
        wait_for(rs_in.at[t], rs_recv.at[t])
        total = total + jnp.sum(rs_in[t].astype(f32), axis=0)
        scaled = total * gain_row
        inner = jnp.mean(scaled * normed, axis=-1, keepdims=True)
        result = (incoming_own + inverse_rms * (scaled - normed * inner)).astype(bf16)
        out_v[t] = result
        if t + 1 < ticks:
            @pl.when(section > 0)
            def _():
                remote(out_v.at[t], up.at[t], up_send.at[t], up_recv.at[t], below, me).start()

            @pl.when(section < sections - 1)
            def _():
                wait_for(up.at[t], up_recv.at[t])
                own[t + 1] = up[t]

            send_incoming(t + 1, own.at[t + 1])
            forward(inc_all, t + 1, ag_recv, agf_send, agf_recv)

    for t in range(ticks):
        out[t] = out_v[t, 0:rows]
    for t in range(ticks):
        wait_for(x_all.at[t, pl.ds(0, places)], x_send.at[t])
        wait_for(x_all.at[t, pl.ds(0, places - 1)], ag_send.at[t])
        wait_for(core_in.at[t], core_send.at[t])
        wait_for(rs_in.at[t], rs_send.at[t])
    for t in range(ticks - 1):
        @pl.when(section > 0)
        def _():
            wait_for(up.at[t], up_send.at[t])


def solution(mesh):
    sections, tps = mesh.shape["section"], mesh.shape["tp"]

    def body(stash, w_in, w_out, gain, plan, arriving, fresh):
        stash, w_in, w_out, arriving = stash[0], w_in[0], w_out[0], arriving[0]
        slots, rows, width = stash.shape
        ticks = plan.shape[0]
        units = w_out.shape[0]
        places = tps // 2
        vmem = pl.BlockSpec(memory_space=pltpu.VMEM)
        hbm = pl.BlockSpec(memory_space=pl.ANY)
        dma = pltpu.SemaphoreType.DMA((ticks,))
        results = pl.pallas_call(
            functools.partial(window_kernel, sections, tps, ticks),
            out_shape=jax.ShapeDtypeStruct((ticks, rows, width), bf16),
            in_specs=[pl.BlockSpec(memory_space=pltpu.SMEM), hbm, hbm, hbm, vmem, vmem, vmem],
            out_specs=vmem,
            scratch_shapes=[
                pltpu.VMEM((width, units), bf16),
                pltpu.VMEM((units, width), bf16),
                pltpu.VMEM((slots, rows, width), bf16),
                pltpu.VMEM((ticks, PAD, width), bf16),
                pltpu.VMEM((ticks, PAD, width), bf16),
                pltpu.VMEM((ticks, tps, PAD, width), bf16),
                pltpu.VMEM((ticks, tps, PAD, width), bf16),
                pltpu.VMEM((ticks, tps * PAD, units), f32),
                pltpu.VMEM((tps * PAD, units), bf16),
                pltpu.VMEM((tps, PAD, width), f32),
                pltpu.VMEM((ticks, tps, PAD, width), bf16),
                pltpu.VMEM((ticks, places, PAD, width), bf16),
                pltpu.VMEM((ticks, places, PAD, width), bf16),
                pltpu.VMEM((ticks, places - 1, PAD, width), bf16),
                pltpu.VMEM((ticks, PAD, width), bf16),
                pltpu.VMEM((ticks - 1, PAD, width), bf16),
                pltpu.SemaphoreType.DMA((3,)),
            ] + [dma] * 12 + [pltpu.SemaphoreType.DMA((ticks - 1,))] * 2,
            compiler_params=pltpu.CompilerParams(
                collective_id=0, has_side_effects=True, vmem_limit_bytes=60 * 2**20),
            name="window",
        )(plan, stash, w_in, w_out, gain, arriving, fresh)
        return results[:, None]

    placed = (
        P("section", None, "tp", None),
        P("section", None, "tp"),
        P("section", "tp", None),
        P("section", None),
        P(),
        P("section", "tp", None),
        P(None, "tp", None),
    )
    return jax.shard_map(
        body, mesh=mesh, in_specs=placed, out_specs=P(None, "section", "tp", None), check_vma=False
    )
```

time: 224 us -> 91.8 us (0.41)
  the two profiles are of different devices: /device:TPU:96 before, /device:TPU:1 now
where the time goes in v1:
time: 91.8 us; the launch traced here: 91.4 us
  Pallas kernels  86.9 us (95%)
  local copies, waits for them, and re-layouts  4.54 us (5%)
    pallas_call x1, Pallas kernels, body(): pl.pallas_call(functools.partial(window_kernel, sections, tps, ticks), ou...  86.9 us
    unnamed x3, local copies, waits for them, and re-layouts  4.54 us

profile of v1, /device:TPU:1, one launch (start us, length us, event | category | flops | bytes accessed | tf_op | source)
XLA Modules:
  0.0 91.4 jit_solution(1946147466907035308)
XLA Ops:
  0.0 1.4 %copy.9.fresh = bf16[2,12,1024]{2,1,0:T(8,128)(2,1)} copy(bf16[2,12,1024]{2,0,1:T(2,128)(2,1)} %param.13) | data formatting | bytes 98304 | tf_op args[6]
  1.4 1.6 %copy.12 = bf16[1,4,12,1024]{3,2,1,0:T(8,128)(2,1)} copy(bf16[1,4,12,1024]{3,1,2,0:T(4,128)(2,1)} %param.7) | data formatting | bytes 196608 | tf_op args[0]
  3.0 86.9 %window.1 = bf16[3,12,1024]{2,1,0:T(8,128)(2,1)} custom-call(s32[3,8]{1,0:T(4,128)} %plan.1, bf16[4,12,1024]{2,1,0:T(8,128)(2,1)} %bitcast.11, bf16[1024,4096]{1,0:T(8,128)(2,1)} %bitcast.9, bf16[4096,1024]{1,0:T(8,128)(2,1)} %bitcast.10, f32[1,1024]{1,0:T(1,128)} %gain.1, bf16[12,1024]{1,0:T(8,128)(2,1)} %bitcast.13, bf16[2,12,1024]{2,1,0:T(8,128)(2,1)} %copy.9.fresh), custom_call_target="tpu_custom_call" | custom-call | tf_op jit(solution)/shard_map/window/pallas_call | solution.py:212
  89.9 1.5 %copy.14 = bf16[3,1,12,1024]{3,2,1,0:T(8,128)(2,1)} copy(bf16[3,1,12,1024]{3,2,1,0:T(8,128)(2,1)} %bitcast.12) | data formatting | bytes 147456

commit v2 on v1

v2 whole, which is shorter than its diff:
```python
import functools

import jax
import jax.numpy as jnp
from jax import lax
from jax.experimental import pallas as pl
from jax.experimental.pallas import tpu as pltpu
from jax.sharding import PartitionSpec as P

epsilon = 1e-06
contract_last = (((1,), (1,)), ((), ()))
bf16, f32 = jnp.bfloat16, jnp.float32
PAD = 16
IN_TILE = 512
BLOCK = 256
LANES = 128
SUB = 8
WIRE = BLOCK + LANES
FAR_FIRST = (5, 7, 1, 3, 4, 6, 2)
FLIPPED = (5, 7, 1, 3)
NEAR = (4, 6, 2)


def packed(value):
    low = value[:, SUB:, :LANES]
    high = pltpu.roll(value[:, SUB:, LANES:], 4, 1)
    row = lax.broadcasted_iota(jnp.int32, low.shape, 1)
    return jnp.concatenate([value[:, :SUB], jnp.where(row < 4, low, high)], axis=2)


def unpacked(wire):
    wire = wire.astype(f32)
    tail = wire[:, :, BLOCK:]
    bottom = jnp.concatenate([tail, pltpu.roll(tail, 4, 1)], axis=2)
    return jnp.concatenate([wire[:, :, :BLOCK], bottom], axis=1)


def window_kernel(
    sections, tps, ticks,
    plan, stash, w_in, w_out, gain, arriving, fresh, out,
    wi, wo, picks, x_all, inc_all, factor, back_sum, hidden, acc, part, core_in, half, rs_in, out_v, pad_v,
    load_sem, x_send, x_recv, xf_send, xf_recv, ag_send, ag_recv, agf_send, agf_recv,
    core_send, core_recv, rs_send, rs_recv, up_send, up_recv, top_send,
):
    section = lax.axis_index("section")
    me = lax.axis_index("tp")
    core = lax.rem(me, 2)
    place = me // 2
    places = tps // 2
    rows, slots, width = stash.shape
    units = wo.shape[0]
    blocks = width // BLOCK
    mirror = lax.rem(section + sections // 2, sections)
    above = lax.rem(section + 1, sections)
    below = lax.rem(section + sections - 1, sections)
    mine = pl.multiple_of(core * places, places)
    theirs = pl.multiple_of((1 - core) * places, places)
    own = mine + place
    partner = me + 1 - 2 * core

    def remote(src, dst, send, recv, to_section, to_tp):
        return pltpu.make_async_remote_copy(
            src_ref=src, dst_ref=dst, send_sem=send, recv_sem=recv,
            device_id={"section": to_section, "tp": to_tp}, device_id_type=pl.DeviceIdType.MESH)

    def wait_for(ref, sem):
        pltpu.make_async_copy(ref, ref, sem).wait()

    def at_place(k):
        return lax.bitwise_xor(place, k) * 2 + core

    def cols_of(b):
        return slice(b * BLOCK, (b + 1) * BLOCK)

    loads = [
        pltpu.make_async_copy(w_in, wi, load_sem.at[0]),
        pltpu.make_async_copy(w_out, wo, load_sem.at[1]),
    ]
    loads[0].start()

    barrier = pltpu.get_barrier_semaphore()

    def greet(to_section, to_tp):
        pl.semaphore_signal(barrier, inc=1, device_id={"section": to_section, "tp": to_tp},
                            device_id_type=pl.DeviceIdType.MESH)

    for k in FAR_FIRST:
        greet(section, at_place(k))
    for k in FAR_FIRST + (0,):
        greet(mirror, at_place(k))
    for k in FLIPPED + (0,):
        greet(above, at_place(k))
        greet(below, at_place(k))
    greet(section, partner)

    pad_v[...] = jnp.zeros_like(pad_v)

    def wire_blocks(value):
        pad_v[0:rows] = value.astype(f32)
        return [packed(pad_v[:, cols_of(b)][None])[0].astype(bf16) for b in range(blocks)]

    def set_own(t, value):
        for b, block in enumerate(wire_blocks(value)):
            inc_all[t, b, own] = block

    def set_pick(t):
        slot = plan[t, mirror]
        pick = stash[:, 0, :]
        for k in range(1, slots):
            pick = jnp.where(slot == k, stash[:, k, :], pick)
        for b, block in enumerate(wire_blocks(pick)):
            picks[t, b] = block

    set_pick(0)
    set_own(0, arriving[...])
    pl.semaphore_wait(barrier, 2 * places + 2 * (1 + len(FLIPPED)))

    def send_x(t):
        for b in range(blocks):
            for k in FAR_FIRST + (0,):
                remote(picks.at[t, b], x_all.at[t, b, own], x_send.at[t], x_recv.at[t, b],
                       mirror, at_place(k)).start()

    def send_own(t, b, to_places, send):
        for k in to_places:
            remote(inc_all.at[t, b, own], inc_all.at[t, b, own], send, ag_recv.at[t, b],
                   section, at_place(k)).start()

    def forward_x(t, b):
        block = x_all.at[t, b, pl.ds(mine, places)]
        wait_for(block, x_recv.at[t, b])
        remote(block, block, xf_send.at[t], xf_recv.at[t, b], section, partner).start()

    def forward_incoming(t, b):
        wait_for(inc_all.at[t, b, pl.ds(0, places - 1)], ag_recv.at[t, b])
        block = inc_all.at[t, b, pl.ds(mine, places)]
        remote(block, block, agf_send.at[t], agf_recv.at[t, b], section, partner).start()

    gain_row = gain[...]

    def preact(t, b, scale_in, scale_out):
        values = unpacked(x_all[t, b]).reshape(tps * PAD, BLOCK)
        if scale_in is not None:
            values = values * scale_in
        inputs = (values * gain_row[:, cols_of(b)]).astype(bf16)
        for n in range(units // IN_TILE):
            cols = slice(n * IN_TILE, (n + 1) * IN_TILE)
            pre = jnp.dot(inputs, wi[cols_of(b), cols], preferred_element_type=f32)
            if b > 0:
                pre = pre + factor[:, cols]
            if b == blocks - 1:
                pre = scale_out * jnp.maximum(pre, 0.0)
            factor[:, cols] = pre

    def x_square(t, b):
        wait_for(x_all.at[t, b, pl.ds(theirs, places)], xf_recv.at[t, b])
        values = unpacked(x_all[t, b]).reshape(tps * PAD, BLOCK)
        return jnp.sum(values * values, axis=-1, keepdims=True)

    def rms_of(square):
        return lax.rsqrt(square * (1.0 / width) + epsilon)

    def first_matmul(t, b):
        wait_for(inc_all.at[t, b, pl.ds(theirs, places)], agf_recv.at[t, b])
        incoming = unpacked(inc_all[t, b]).reshape(tps * PAD, BLOCK).astype(bf16)
        for n in range(units // IN_TILE):
            cols = slice(n * IN_TILE, (n + 1) * IN_TILE)
            back = lax.dot_general(incoming, wo[cols, cols_of(b)], contract_last, preferred_element_type=f32)
            if b > 0:
                back = back + back_sum[:, cols]
            if b == blocks - 1:
                hidden[:, cols] = (back * factor[:, cols]).astype(bf16)
            else:
                back_sum[:, cols] = back

    def second_matmul(t, b):
        total = lax.dot_general(hidden[...], wi[cols_of(b), :], contract_last, preferred_element_type=f32)
        total = packed(total.reshape(tps, PAD, BLOCK))
        acc[b] = total
        part[t, b] = total.astype(bf16)
        remote(part.at[t, b, pl.ds(theirs, places)], core_in.at[t, b], core_send.at[t], core_recv.at[t, b],
               section, partner).start()

    def scatter(t, b):
        wait_for(core_in.at[t, b], core_recv.at[t, b])
        half[t, b] = (acc[b, pl.ds(mine, places)] + core_in[t, b].astype(f32)).astype(bf16)
        for k in FAR_FIRST:
            remote(half.at[t, b, lax.bitwise_xor(place, k)], rs_in.at[t, b, k - 1], rs_send.at[t], rs_recv.at[t, b],
                   section, at_place(k)).start()

    send_x(0)
    for b in range(blocks):
        send_own(0, b, FAR_FIRST, ag_send.at[0])
    loads[1].start()
    for t in range(1, ticks):
        set_pick(t)

    @pl.when(section == sections - 1)
    def _():
        for t in range(1, ticks):
            set_own(t, fresh[:, t - 1, :])

    forward_x(0, 0)
    forward_x(0, 1)
    loads[0].wait()
    for b in range(blocks):
        if b + 2 < blocks:
            forward_x(0, b + 2)
        else:
            forward_incoming(0, b + 2 - blocks)
        square = x_square(0, b) if b == 0 else square + x_square(0, b)
        preact(0, b, None, 2.0 * rms_of(square) if b == blocks - 1 else None)

    loads[1].wait()
    for t in range(ticks):
        if t > 0:
            forward_incoming(t, 0)
            forward_incoming(t, 1)
        for b in range(blocks):
            first_matmul(t, b)
            if b + 2 < blocks:
                forward_incoming(t, b + 2)
        second_matmul(t, 0)
        second_matmul(t, 1)
        for b in range(2, blocks):
            second_matmul(t, b)
            scatter(t, b - 2)
        scatter(t, blocks - 2)
        scatter(t, blocks - 1)
        if t + 1 < ticks:
            send_x(t + 1)
        values = jnp.concatenate([unpacked(x_all[t, b, pl.ds(own, 1)])[0] for b in range(blocks)], axis=1)
        inverse_rms = lax.rsqrt(jnp.mean(values * values, axis=-1, keepdims=True) + epsilon)
        normed = values * inverse_rms
        incoming = jnp.concatenate([unpacked(inc_all[t, b, pl.ds(own, 1)])[0] for b in range(blocks)], axis=1)
        scaled = []
        for b in range(blocks):
            wait_for(rs_in.at[t, b], rs_recv.at[t, b])
            total = (acc[b, pl.ds(own, 1)] + core_in[t, b, pl.ds(place, 1)].astype(f32)
                     + jnp.sum(rs_in[t, b].astype(f32), axis=0, keepdims=True))
            scaled.append(unpacked(total)[0] * gain_row[:, cols_of(b)])
        scaled = jnp.concatenate(scaled, axis=1)
        inner = jnp.mean(scaled * normed, axis=-1, keepdims=True)
        result = incoming + inverse_rms * (scaled - normed * inner)
        if t + 1 < ticks:
            for b in range(blocks):
                out_v[t, b] = packed(result[:, cols_of(b)][None])[0].astype(bf16)

            @pl.when(section > 0)
            def _():
                for b in range(blocks):
                    remote(out_v.at[t, b], inc_all.at[t + 1, b, own], up_send.at[t], up_recv.at[t, b], below, me).start()
                    for k in FLIPPED:
                        remote(out_v.at[t, b], inc_all.at[t + 1, b, own], up_send.at[t], ag_recv.at[t + 1, b],
                               below, at_place(k)).start()

            @pl.when(section == sections - 1)
            def _():
                for b in range(blocks):
                    send_own(t + 1, b, FLIPPED, top_send.at[t])

        out[t] = result[0:rows].astype(bf16)
        if t + 1 < ticks:
            for b in range(blocks):
                forward_x(t + 1, b)
            for b in range(blocks):
                @pl.when(section < sections - 1)
                def _():
                    wait_for(inc_all.at[t + 1, b, own], up_recv.at[t, b])

                send_own(t + 1, b, NEAR, ag_send.at[t + 1])

            square = x_square(t + 1, 0)
            for b in range(1, blocks):
                square = square + x_square(t + 1, b)
            for b in range(blocks):
                preact(t + 1, b, rms_of(square), 2.0)

    def sent(t, copies, sem):
        wait_for(inc_all.at[t, pl.ds(0, blocks), pl.ds(0, copies)], sem)

    for t in range(ticks):
        wait_for(x_all.at[t, pl.ds(0, blocks), pl.ds(0, places)], x_send.at[t])
        wait_for(x_all.at[t, pl.ds(0, blocks), pl.ds(0, places)], xf_send.at[t])
        sent(t, len(FAR_FIRST) if t == 0 else len(NEAR), ag_send.at[t])
        sent(t, places, agf_send.at[t])
        wait_for(core_in.at[t], core_send.at[t])
        wait_for(rs_in.at[t], rs_send.at[t])
    for t in range(ticks - 1):
        @pl.when(section > 0)
        def _():
            sent(t, 1 + len(FLIPPED), up_send.at[t])

        @pl.when(section == sections - 1)
        def _():
            sent(t, len(FLIPPED), top_send.at[t])


def solution(mesh):
    sections, tps = mesh.shape["section"], mesh.shape["tp"]

    def body(stash, w_in, w_out, gain, plan, arriving, fresh):
        stash, w_in, w_out, arriving = stash[0], w_in[0], w_out[0], arriving[0]
        stash, fresh = jnp.swapaxes(stash, 0, 1), jnp.swapaxes(fresh, 0, 1)
        rows, slots, width = stash.shape
        ticks = plan.shape[0]
        units = w_out.shape[0]
        places = tps // 2
        blocks = width // BLOCK
        vmem = pl.BlockSpec(memory_space=pltpu.VMEM)
        hbm = pl.BlockSpec(memory_space=pl.ANY)
        each = pltpu.SemaphoreType.DMA((ticks,))
        each_block = pltpu.SemaphoreType.DMA((ticks, blocks))
        results = pl.pallas_call(
            functools.partial(window_kernel, sections, tps, ticks),
            out_shape=jax.ShapeDtypeStruct((ticks, rows, width), bf16),
            in_specs=[pl.BlockSpec(memory_space=pltpu.SMEM), vmem, hbm, hbm, vmem, vmem, vmem],
            out_specs=vmem,
            scratch_shapes=[
                pltpu.VMEM((width, units), bf16),
                pltpu.VMEM((units, width), bf16),
                pltpu.VMEM((ticks, blocks, SUB, WIRE), bf16),
                pltpu.VMEM((ticks, blocks, tps, SUB, WIRE), bf16),
                pltpu.VMEM((ticks, blocks, tps, SUB, WIRE), bf16),
                pltpu.VMEM((tps * PAD, units), f32),
                pltpu.VMEM((tps * PAD, units), f32),
                pltpu.VMEM((tps * PAD, units), bf16),
                pltpu.VMEM((blocks, tps, SUB, WIRE), f32),
                pltpu.VMEM((ticks, blocks, tps, SUB, WIRE), bf16),
                pltpu.VMEM((ticks, blocks, places, SUB, WIRE), bf16),
                pltpu.VMEM((ticks, blocks, places, SUB, WIRE), bf16),
                pltpu.VMEM((ticks, blocks, places - 1, SUB, WIRE), bf16),
                pltpu.VMEM((ticks, blocks, SUB, WIRE), bf16),
                pltpu.VMEM((PAD, width), f32),
                pltpu.SemaphoreType.DMA((2,)),
                each, each_block, each, each_block,
                each, each_block, each, each_block,
                each, each_block, each, each_block,
                each, each_block, each,
            ],
            compiler_params=pltpu.CompilerParams(
                collective_id=0, has_side_effects=True, vmem_limit_bytes=60 * 2**20),
            name="window",
        )(plan, stash, w_in, w_out, gain, arriving, fresh)
        return results[:, None]

    placed = (
        P("section", None, "tp", None),
        P("section", None, "tp"),
        P("section", "tp", None),
        P("section", None),
        P(),
        P("section", "tp", None),
        P(None, "tp", None),
    )
    return jax.shard_map(
        body, mesh=mesh, in_specs=placed, out_specs=P(None, "section", "tp", None), check_vma=False
    )
```

time: 91.8 us -> 79.3 us (0.86)
  Pallas kernels: 86.9 us -> 77.6 us
  local copies, waits for them, and re-layouts: 4.54 us -> 1.54 us
    pallas_call x1, Pallas kernels: 86.9 us -> 77.6 us  [body(): pl.pallas_call(functools.partial(window_kernel, sections, tps, ticks), ou...]
    unnamed x3 -> x1, local copies, waits for them, and re-layouts: 4.54 us -> 1.54 us
where the time goes in v2:
time: 79.3 us; the launch traced here: 79.1 us
  Pallas kernels  77.6 us (98%)
  local copies, waits for them, and re-layouts  1.54 us (2%)
    pallas_call x1, Pallas kernels, body(): pl.pallas_call(functools.partial(window_kernel, sections, tps, ticks), ou...  77.6 us

profile of v2, /device:TPU:1, one launch (start us, length us, event | category | flops | bytes accessed | tf_op | source)
XLA Modules:
  0.0 79.1 jit_solution(14170009668027424269)
XLA Ops:
  0.0 77.6 %window.1 = bf16[3,12,1024]{2,1,0:T(8,128)(2,1)} custom-call(s32[3,8]{1,0:T(4,128)} %plan.1, bf16[12,4,1024]{2,1,0:T(4,128)(2,1)} %bitcast.13, bf16[1024,4096]{1,0:T(8,128)(2,1)} %bitcast.10, bf16[4096,1024]{1,0:T(8,128)(2,1)} %bitcast.11, f32[1,1024]{1,0:T(1,128)} %gain.1, bf16[12,1024]{1,0:T(8,128)(2,1)} %bitcast.15, bf16[12,2,1024]{2,1,0:T(2,128)(2,1)} %bitcast.14), custom_call_target="tpu_custom_call" | custom-call | tf_op jit(solution)/shard_map/window/pallas_call | solution.py:314
  77.6 1.5 %copy.10 = bf16[3,1,12,1024]{3,2,1,0:T(8,128)(2,1)} copy(bf16[3,1,12,1024]{3,2,1,0:T(8,128)(2,1)} %bitcast.12) | data formatting | bytes 147456

commit v3 on v2

--- a/solution.py
+++ b/solution.py
@@ -19,6 +19,7 @@
 FAR_FIRST = (5, 7, 1, 3, 4, 6, 2)
 FLIPPED = (5, 7, 1, 3)
 NEAR = (4, 6, 2)
+AHEAD = 3
 
 
 def packed(value):
@@ -37,8 +38,8 @@
 
 def window_kernel(
     sections, tps, ticks,
-    plan, stash, w_in, w_out, gain, arriving, fresh, out,
-    wi, wo, picks, x_all, inc_all, factor, back_sum, hidden, acc, part, core_in, half, rs_in, out_v, pad_v,
+    plan_in, stash_in, w_in, w_out, gain_in, arriving_in, fresh_in, out,
+    plan, stash, gain, arriving, fresh, wi, wo, picks, x_all, inc_all, factor, back_sum, hidden, raw, acc, part, core_in, half, rs_in, out_v, pad_v,
     load_sem, x_send, x_recv, xf_send, xf_recv, ag_send, ag_recv, agf_send, agf_recv,
     core_send, core_recv, rs_send, rs_recv, up_send, up_recv, top_send,
 ):
@@ -72,12 +73,6 @@
     def cols_of(b):
         return slice(b * BLOCK, (b + 1) * BLOCK)
 
-    loads = [
-        pltpu.make_async_copy(w_in, wi, load_sem.at[0]),
-        pltpu.make_async_copy(w_out, wo, load_sem.at[1]),
-    ]
-    loads[0].start()
-
     barrier = pltpu.get_barrier_semaphore()
 
     def greet(to_section, to_tp):
@@ -93,7 +88,13 @@
         greet(below, at_place(k))
     greet(section, partner)
 
+    pairs = ((plan_in, plan), (stash_in, stash), (arriving_in, arriving), (gain_in, gain), (fresh_in, fresh), (w_in, wi), (w_out, wo))
+    loads = [pltpu.make_async_copy(src, dst, load_sem.at[n]) for n, (src, dst) in enumerate(pairs)]
+    for load in loads[:-1]:
+        load.start()
     pad_v[...] = jnp.zeros_like(pad_v)
+    for load in loads[:3]:
+        load.wait()
 
     def wire_blocks(value):
         pad_v[0:rows] = value.astype(f32)
@@ -136,13 +137,11 @@
         block = inc_all.at[t, b, pl.ds(mine, places)]
         remote(block, block, agf_send.at[t], agf_recv.at[t, b], section, partner).start()
 
-    gain_row = gain[...]
-
     def preact(t, b, scale_in, scale_out):
         values = unpacked(x_all[t, b]).reshape(tps * PAD, BLOCK)
         if scale_in is not None:
             values = values * scale_in
-        inputs = (values * gain_row[:, cols_of(b)]).astype(bf16)
+        inputs = (values * gain[:, cols_of(b)]).astype(bf16)
         for n in range(units // IN_TILE):
             cols = slice(n * IN_TILE, (n + 1) * IN_TILE)
             pre = jnp.dot(inputs, wi[cols_of(b), cols], preferred_element_type=f32)
@@ -173,17 +172,25 @@
             else:
                 back_sum[:, cols] = back
 
-    def second_matmul(t, b):
-        total = lax.dot_general(hidden[...], wi[cols_of(b), :], contract_last, preferred_element_type=f32)
-        total = packed(total.reshape(tps, PAD, BLOCK))
+    def second_matmul(b):
+        raw[b] = lax.dot_general(hidden[...], wi[cols_of(b), :], contract_last, preferred_element_type=f32)
+
+    def pack_part(t, b):
+        total = packed(raw[b].reshape(tps, PAD, BLOCK))
         acc[b] = total
         part[t, b] = total.astype(bf16)
+
+    def send_part(t, b):
         remote(part.at[t, b, pl.ds(theirs, places)], core_in.at[t, b], core_send.at[t], core_recv.at[t, b],
                section, partner).start()
 
+    def take_part(t, b):
+        wait_for(core_in.at[t, b], core_recv.at[t, b])
+
+    def pack_half(t, b):
+        half[t, b] = (acc[b, pl.ds(mine, places)] + core_in[t, b].astype(f32)).astype(bf16)
+
     def scatter(t, b):
-        wait_for(core_in.at[t, b], core_recv.at[t, b])
-        half[t, b] = (acc[b, pl.ds(mine, places)] + core_in[t, b].astype(f32)).astype(bf16)
         for k in FAR_FIRST:
             remote(half.at[t, b, lax.bitwise_xor(place, k)], rs_in.at[t, b, k - 1], rs_send.at[t], rs_recv.at[t, b],
                    section, at_place(k)).start()
@@ -191,42 +198,53 @@
     send_x(0)
     for b in range(blocks):
         send_own(0, b, FAR_FIRST, ag_send.at[0])
-    loads[1].start()
+    loads[6].start()
     for t in range(1, ticks):
         set_pick(t)
+    loads[3].wait()
+    loads[4].wait()
 
     @pl.when(section == sections - 1)
     def _():
         for t in range(1, ticks):
             set_own(t, fresh[:, t - 1, :])
 
-    forward_x(0, 0)
-    forward_x(0, 1)
-    loads[0].wait()
+    for b in range(AHEAD):
+        forward_x(0, b)
+    loads[5].wait()
     for b in range(blocks):
-        if b + 2 < blocks:
-            forward_x(0, b + 2)
-        else:
-            forward_incoming(0, b + 2 - blocks)
         square = x_square(0, b) if b == 0 else square + x_square(0, b)
         preact(0, b, None, 2.0 * rms_of(square) if b == blocks - 1 else None)
-
-    loads[1].wait()
+        if b + AHEAD < blocks:
+            forward_x(0, b + AHEAD)
+        else:
+            forward_incoming(0, b + AHEAD - blocks)
+    loads[6].wait()
     for t in range(ticks):
         if t > 0:
-            forward_incoming(t, 0)
-            forward_incoming(t, 1)
+            for b in range(AHEAD):
+                forward_incoming(t, b)
         for b in range(blocks):
             first_matmul(t, b)
-            if b + 2 < blocks:
-                forward_incoming(t, b + 2)
-        second_matmul(t, 0)
-        second_matmul(t, 1)
-        for b in range(2, blocks):
-            second_matmul(t, b)
-            scatter(t, b - 2)
-        scatter(t, blocks - 2)
-        scatter(t, blocks - 1)
+            if b + AHEAD < blocks:
+                forward_incoming(t, b + AHEAD)
+        second_matmul(0)
+        for b in range(1, blocks):
+            second_matmul(b)
+            pack_part(t, b - 1)
+            if b > 2:
+                pack_half(t, b - 3)
+            send_part(t, b - 1)
+            if b > 2:
+                scatter(t, b - 3)
+            if b > 1 and b < blocks - 1:
+                take_part(t, b - 2)
+        pack_part(t, blocks - 1)
+        send_part(t, blocks - 1)
+        for b in range(blocks - 3, blocks):
+            take_part(t, b)
+            pack_half(t, b)
+            scatter(t, b)
         if t + 1 < ticks:
             send_x(t + 1)
         values = jnp.concatenate([unpacked(x_all[t, b, pl.ds(own, 1)])[0] for b in range(blocks)], axis=1)
@@ -238,7 +256,7 @@
             wait_for(rs_in.at[t, b], rs_recv.at[t, b])
             total = (acc[b, pl.ds(own, 1)] + core_in[t, b, pl.ds(place, 1)].astype(f32)
                      + jnp.sum(rs_in[t, b].astype(f32), axis=0, keepdims=True))
-            scaled.append(unpacked(total)[0] * gain_row[:, cols_of(b)])
+            scaled.append(unpacked(total)[0] * gain[:, cols_of(b)])
         scaled = jnp.concatenate(scaled, axis=1)
         inner = jnp.mean(scaled * normed, axis=-1, keepdims=True)
         result = incoming + inverse_rms * (scaled - normed * inner)
@@ -313,10 +331,15 @@
         each_block = pltpu.SemaphoreType.DMA((ticks, blocks))
         results = pl.pallas_call(
             functools.partial(window_kernel, sections, tps, ticks),
-            out_shape=jax.ShapeDtypeStruct((ticks, rows, width), bf16),
-            in_specs=[pl.BlockSpec(memory_space=pltpu.SMEM), vmem, hbm, hbm, vmem, vmem, vmem],
+            out_shape=pltpu.VMEM((ticks, rows, width), bf16),
+            in_specs=[hbm] * 7,
             out_specs=vmem,
             scratch_shapes=[
+                pltpu.SMEM(plan.shape, plan.dtype),
+                pltpu.VMEM(stash.shape, bf16),
+                pltpu.VMEM(gain.shape, f32),
+                pltpu.VMEM(arriving.shape, bf16),
+                pltpu.VMEM(fresh.shape, bf16),
                 pltpu.VMEM((width, units), bf16),
                 pltpu.VMEM((units, width), bf16),
                 pltpu.VMEM((ticks, blocks, SUB, WIRE), bf16),
@@ -325,6 +348,7 @@
                 pltpu.VMEM((tps * PAD, units), f32),
                 pltpu.VMEM((tps * PAD, units), f32),
                 pltpu.VMEM((tps * PAD, units), bf16),
+                pltpu.VMEM((blocks, tps * PAD, BLOCK), f32),
                 pltpu.VMEM((blocks, tps, SUB, WIRE), f32),
                 pltpu.VMEM((ticks, blocks, tps, SUB, WIRE), bf16),
                 pltpu.VMEM((ticks, blocks, places, SUB, WIRE), bf16),
@@ -332,7 +356,7 @@
                 pltpu.VMEM((ticks, blocks, places - 1, SUB, WIRE), bf16),
                 pltpu.VMEM((ticks, blocks, SUB, WIRE), bf16),
                 pltpu.VMEM((PAD, width), f32),
-                pltpu.SemaphoreType.DMA((2,)),
+                pltpu.SemaphoreType.DMA((7,)),
                 each, each_block, each, each_block,
                 each, each_block, each, each_block,
                 each, each_block, each, each_block,

time: 79.3 us -> 74 us (0.933)
  Pallas kernels: 77.6 us -> 73.3 us
  local copies, waits for them, and re-layouts: 1.54 us -> 0.64 us
    pallas_call x1, Pallas kernels: 77.6 us -> 73.3 us  [body(): pl.pallas_call(functools.partial(window_kernel, sections, tps, ticks), ou...]
    unnamed x1, local copies, waits for them, and re-layouts: 1.54 us -> 0.64 us
where the time goes in v3:
time: 74 us; the launch traced here: 73.9 us
  Pallas kernels  73.3 us (99%)
    pallas_call x1, Pallas kernels, body(): pl.pallas_call(functools.partial(window_kernel, sections, tps, ticks), ou...  73.3 us

profile of v3, /device:TPU:1, one launch (start us, length us, event | category | flops | bytes accessed | tf_op | source)
XLA Modules:
  0.0 73.9 jit_solution(7455378045778180333)
XLA Ops:
  0.0 73.3 %window.1 = bf16[3,12,1024]{2,1,0:T(8,128)(2,1)S(1)} custom-call(s32[3,8]{1,0:T(4,128)} %plan_in.1, bf16[12,4,1024]{2,1,0:T(4,128)(2,1)} %bitcast.13, bf16[1024,4096]{1,0:T(8,128)(2,1)} %bitcast.11, bf16[4096,1024]{1,0:T(8,128)(2,1)} %bitcast.12, f32[1,1024]{1,0:T(1,128)} %gain_in.1, bf16[12,1024]{1,0:T(8,128)(2,1)} %bitcast.15, bf16[12,2,1024]{2,1,0:T(2,128)(2,1)} %bitcast.14), custom_call_target="tpu_custom_call" | custom-call | tf_op jit(solution)/shard_map/window/pallas_call | solution.py:332
  73.3 0.6 copy.10

commit v4 on v3

--- a/solution.py
+++ b/solution.py
@@ -17,8 +17,8 @@
 SUB = 8
 WIRE = BLOCK + LANES
 FAR_FIRST = (5, 7, 1, 3, 4, 6, 2)
-FLIPPED = (5, 7, 1, 3)
-NEAR = (4, 6, 2)
+FLIPPED = (5, 7, 3)
+NEAR = (1, 4, 6, 2)
 AHEAD = 3
 
 
@@ -116,11 +116,21 @@
     set_own(0, arriving[...])
     pl.semaphore_wait(barrier, 2 * places + 2 * (1 + len(FLIPPED)))
 
-    def send_x(t):
-        for b in range(blocks):
+    def send_x(t, parts):
+        for b in parts:
             for k in FAR_FIRST + (0,):
                 remote(picks.at[t, b], x_all.at[t, b, own], x_send.at[t], x_recv.at[t, b],
                        mirror, at_place(k)).start()
+
+    def send_x_whole(t):
+        for k in FAR_FIRST + (0,):
+            remote(picks.at[t], x_all.at[t, pl.ds(0, blocks), own], x_send.at[t], x_recv.at[t, 0],
+                   mirror, at_place(k)).start()
+
+    def forward_x_whole(t):
+        block = x_all.at[t, pl.ds(0, blocks), pl.ds(mine, places)]
+        wait_for(block, x_recv.at[t, 0])
+        remote(block, block, xf_send.at[t], xf_recv.at[t, 0], section, partner).start()
 
     def send_own(t, b, to_places, send):
         for k in to_places:
@@ -153,6 +163,9 @@
 
     def x_square(t, b):
         wait_for(x_all.at[t, b, pl.ds(theirs, places)], xf_recv.at[t, b])
+        return row_square(t, b)
+
+    def row_square(t, b):
         values = unpacked(x_all[t, b]).reshape(tps * PAD, BLOCK)
         return jnp.sum(values * values, axis=-1, keepdims=True)
 
@@ -195,7 +208,7 @@
             remote(half.at[t, b, lax.bitwise_xor(place, k)], rs_in.at[t, b, k - 1], rs_send.at[t], rs_recv.at[t, b],
                    section, at_place(k)).start()
 
-    send_x(0)
+    send_x(0, range(blocks))
     for b in range(blocks):
         send_own(0, b, FAR_FIRST, ag_send.at[0])
     loads[6].start()
@@ -220,14 +233,17 @@
         else:
             forward_incoming(0, b + AHEAD - blocks)
     loads[6].wait()
-    for t in range(ticks):
-        if t > 0:
-            for b in range(AHEAD):
-                forward_incoming(t, b)
+
+    def tick(t, carry):
+        more = t + 1 < ticks
         for b in range(blocks):
             first_matmul(t, b)
             if b + AHEAD < blocks:
                 forward_incoming(t, b + AHEAD)
+            if b == 0:
+                @pl.when(more)
+                def _():
+                    send_x_whole(t + 1)
         second_matmul(0)
         for b in range(1, blocks):
             second_matmul(b)
@@ -245,8 +261,6 @@
             take_part(t, b)
             pack_half(t, b)
             scatter(t, b)
-        if t + 1 < ticks:
-            send_x(t + 1)
         values = jnp.concatenate([unpacked(x_all[t, b, pl.ds(own, 1)])[0] for b in range(blocks)], axis=1)
         inverse_rms = lax.rsqrt(jnp.mean(values * values, axis=-1, keepdims=True) + epsilon)
         normed = values * inverse_rms
@@ -260,27 +274,28 @@
         scaled = jnp.concatenate(scaled, axis=1)
         inner = jnp.mean(scaled * normed, axis=-1, keepdims=True)
         result = incoming + inverse_rms * (scaled - normed * inner)
-        if t + 1 < ticks:
+        for b in range(blocks):
+            out_v[t, b] = packed(result[:, cols_of(b)][None])[0].astype(bf16)
+
+        @pl.when(jnp.logical_and(more, section > 0))
+        def _():
             for b in range(blocks):
-                out_v[t, b] = packed(result[:, cols_of(b)][None])[0].astype(bf16)
-
-            @pl.when(section > 0)
-            def _():
-                for b in range(blocks):
-                    remote(out_v.at[t, b], inc_all.at[t + 1, b, own], up_send.at[t], up_recv.at[t, b], below, me).start()
-                    for k in FLIPPED:
-                        remote(out_v.at[t, b], inc_all.at[t + 1, b, own], up_send.at[t], ag_recv.at[t + 1, b],
-                               below, at_place(k)).start()
-
-            @pl.when(section == sections - 1)
-            def _():
-                for b in range(blocks):
-                    send_own(t + 1, b, FLIPPED, top_send.at[t])
+                remote(out_v.at[t, b], inc_all.at[t + 1, b, own], up_send.at[t], up_recv.at[t, b], below, me).start()
+            for b in range(blocks):
+                for k in FLIPPED:
+                    remote(out_v.at[t, b], inc_all.at[t + 1, b, own], up_send.at[t], ag_recv.at[t + 1, b],
+                           below, at_place(k)).start()
+
+        @pl.when(jnp.logical_and(more, section == sections - 1))
+        def _():
+            for b in range(blocks):
+                send_own(t + 1, b, FLIPPED, top_send.at[t])
 
         out[t] = result[0:rows].astype(bf16)
-        if t + 1 < ticks:
-            for b in range(blocks):
-                forward_x(t + 1, b)
+
+        @pl.when(more)
+        def _():
+            forward_x_whole(t + 1)
             for b in range(blocks):
                 @pl.when(section < sections - 1)
                 def _():
@@ -288,11 +303,18 @@
 
                 send_own(t + 1, b, NEAR, ag_send.at[t + 1])
 
-            square = x_square(t + 1, 0)
+            wait_for(x_all.at[t + 1, pl.ds(0, blocks), pl.ds(theirs, places)], xf_recv.at[t + 1, 0])
+            square = row_square(t + 1, 0)
             for b in range(1, blocks):
-                square = square + x_square(t + 1, b)
+                square = square + row_square(t + 1, b)
             for b in range(blocks):
                 preact(t + 1, b, rms_of(square), 2.0)
+            for b in range(AHEAD):
+                forward_incoming(t + 1, b)
+
+        return carry
+
+    lax.fori_loop(0, ticks, tick, 0)
 
     def sent(t, copies, sem):
         wait_for(inc_all.at[t, pl.ds(0, blocks), pl.ds(0, copies)], sem)

time: 74 us -> 71.4 us (0.965)
  Pallas kernels: 73.3 us -> 70.6 us
    pallas_call x1, Pallas kernels: 73.3 us -> 70.6 us  [body(): pl.pallas_call(functools.partial(window_kernel, sections, tps, ticks), ou...]
where the time goes in v4:
time: 71.4 us; the launch traced here: 71.3 us
  Pallas kernels  70.6 us (99%)
    pallas_call x1, Pallas kernels, body(): pl.pallas_call(functools.partial(window_kernel, sections, tps, ticks), ou...  70.6 us

profile of v4, /device:TPU:1, one launch (start us, length us, event | category | flops | bytes accessed | tf_op | source)
XLA Modules:
  0.0 71.3 jit_solution(12728509398922064262)
XLA Ops:
  0.0 70.6 %window.1 = bf16[3,12,1024]{2,1,0:T(8,128)(2,1)S(1)} custom-call(s32[3,8]{1,0:T(4,128)} %plan_in.1, bf16[12,4,1024]{2,1,0:T(4,128)(2,1)} %bitcast.13, bf16[1024,4096]{1,0:T(8,128)(2,1)} %bitcast.11, bf16[4096,1024]{1,0:T(8,128)(2,1)} %bitcast.12, f32[1,1024]{1,0:T(1,128)} %gain_in.1, bf16[12,1024]{1,0:T(8,128)(2,1)} %bitcast.15, bf16[12,2,1024]{2,1,0:T(2,128)(2,1)} %bitcast.14), custom_call_target="tpu_custom_call" | custom-call | tf_op jit(solution)/shard_map/window/pallas_call | solution.py:354
  70.6 0.6 copy.10

commit v5 on v4

--- a/solution.py
+++ b/solution.py
@@ -11,7 +11,7 @@
 contract_last = (((1,), (1,)), ((), ()))
 bf16, f32 = jnp.bfloat16, jnp.float32
 PAD = 16
-IN_TILE = 512
+IN_TILE = 1024
 BLOCK = 256
 LANES = 128
 SUB = 8

time: 71.4 us -> 71.4 us (level)
  no operation moved by 1% of the time
where the time goes in v5:
time: 71.4 us; the launch traced here: 71.3 us
  Pallas kernels  70.6 us (99%)
    pallas_call x1, Pallas kernels, body(): pl.pallas_call(functools.partial(window_kernel, sections, tps, ticks), ou...  70.6 us

profile of v5, /device:TPU:1, one launch (start us, length us, event | category | flops | bytes accessed | tf_op | source)
XLA Modules:
  0.0 71.3 jit_solution(12728509398922064262)
XLA Ops:
  0.0 70.6 %window.1 = bf16[3,12,1024]{2,1,0:T(8,128)(2,1)S(1)} custom-call(s32[3,8]{1,0:T(4,128)} %plan_in.1, bf16[12,4,1024]{2,1,0:T(4,128)(2,1)} %bitcast.13, bf16[1024,4096]{1,0:T(8,128)(2,1)} %bitcast.11, bf16[4096,1024]{1,0:T(8,128)(2,1)} %bitcast.12, f32[1,1024]{1,0:T(1,128)} %gain_in.1, bf16[12,1024]{1,0:T(8,128)(2,1)} %bitcast.15, bf16[12,2,1024]{2,1,0:T(2,128)(2,1)} %bitcast.14), custom_call_target="tpu_custom_call" | custom-call | tf_op jit(solution)/shard_map/window/pallas_call | solution.py:354
  70.6 0.6 copy.10
